TPU v7x, 256 devices: a whole 4x4x8 slice. The times are simulated.
256 devices in a mesh: ctx: 8 (over y, x_hi), chan: 32 (over x_lo, z, core).
Axes of the slice: x: 4 (x_hi: 2, x_lo: 2; x = x_hi * 2 + x_lo), y: 4, z: 8, core: 2. Of those that a mesh axis runs over, the one named last changes fastest.
Arguments:
- token_ids: int32 [2048], P('ctx'), may hold values from 0 to 511
- embed_table: bfloat16 [512, 8192], P(None, 'chan'), may hold values from -6 to 6
- in_weight: bfloat16 [8192, 3, 8192], P(None, None, 'chan'), may hold values from -0.0625 to 0.0625
- feat_taps: float32 [3, 3, 8192], P(None, None, 'chan'), may hold values from -3.5 to 3.5
- modal_rates: float32 [16, 512], P(None, 'chan'), may hold values from 4.8828126e-05 to 0.03
- modal_residues: float32 [16, 512], P(None, 'chan'), may hold values from -1.5 to 1.5
- out_grad: bfloat16 [2048, 8192], P('ctx', 'chan'), may hold values from -6 to 6
Outputs:
- output: bfloat16 [2048, 8192], P('ctx', 'chan')
- grad_tokens: bfloat16 [2048, 8192], P('ctx', 'chan')
All inputs are finite; a program needn't handle non-finite values.
Results may differ from a plain program's by a relative error of at most 0.034.
Values may be sent and summed in bfloat16 or wider, within the bound.
No kernel may reach another device: no remote copies, remote signals or barrier semaphores. Data moves between devices by JAX's collectives and lax.ppermute only.
A program may use at most 128 MiB of HBM per device.

v0:
```python
import jax
import jax.numpy as jnp
from jax import lax
from jax.sharding import PartitionSpec as P

GROUP = 16
ORDER = 16
FEAT = 3
exact_mode = lax.Precision.HIGHEST


def passed_along(value, axis, by):
    count = lax.axis_size(axis)
    pairs = [(i, i + by) for i in range(count) if 0 <= i + by < count]
    return lax.ppermute(value, axis, pairs)


def neighbour_rows(pieces, offset):
    return passed_along(pieces, "ctx", offset)


def featurize_local(stream, taps):
    length = stream.shape[0]
    tail_rows = neighbour_rows(stream[length - (FEAT - 1) :], 1)
    widened = jnp.concatenate([tail_rows, stream], axis=0).astype(jnp.float32)
    summed = jnp.zeros(stream.shape, jnp.float32)
    for tap_index in range(FEAT):
        begin = FEAT - 1 - tap_index
        summed = summed + taps[:, tap_index, :][None] * widened[begin : begin + length]
    return summed


def featurize_back(stream, taps):
    length = stream.shape[0]
    head_rows = neighbour_rows(stream[: FEAT - 1], -1)
    widened = jnp.concatenate([stream, head_rows], axis=0).astype(jnp.float32)
    summed = jnp.zeros(stream.shape, jnp.float32)
    for tap_index in range(FEAT):
        summed = summed + taps[:, tap_index, :][None] * widened[tap_index : tap_index + length]
    return summed


def modal_tables(block_rates, block_gains, length):
    positions = jnp.arange(length, dtype=jnp.float32)
    powers = jnp.exp(-positions[:, None, None] * block_rates[None])
    growth = jnp.exp(positions[:, None, None] * block_rates[None])
    weighted = powers * block_gains[None]
    full_table = jnp.einsum("tog,sog->tsg", weighted, growth, precision=exact_mode)
    causal = (
        jnp.arange(length, dtype=jnp.int32)[:, None] >= jnp.arange(length, dtype=jnp.int32)[None, :]
    )
    toeplitz = jnp.where(causal[:, :, None], full_table, 0.0)
    start_weights = weighted * jnp.exp(-block_rates)[None]
    end_powers = jnp.exp(-(float(length - 1) - positions)[:, None, None] * block_rates[None])
    return (toeplitz, start_weights, end_powers)


def modal_block(sequence, tables):
    toeplitz, start_weights, end_powers = tables
    local_part = jnp.einsum("tsg,sgc->tgc", toeplitz, sequence, precision=exact_mode)
    end_state = jnp.einsum("sog,sgc->ogc", end_powers, sequence, precision=exact_mode)
    return (local_part, end_state)


def modal_apply(sequence, modal_rates, modal_residues, backward):
    length, channels = sequence.shape
    groups = channels // GROUP
    gain_terms = modal_residues * jnp.sqrt(-jnp.expm1(-2.0 * modal_rates))
    shaped = sequence.reshape(length, groups, GROUP)
    ctx_devices = lax.axis_size("ctx")
    share_groups = groups // ctx_devices
    exchanged = lax.all_to_all(
        shaped.astype(jnp.bfloat16), "ctx", split_axis=1, concat_axis=0, tiled=True
    ).astype(shaped.dtype)
    first_group = lax.axis_index("ctx") * share_groups
    own_rates = lax.dynamic_slice_in_dim(modal_rates, first_group, share_groups, 1)
    own_gains = lax.dynamic_slice_in_dim(gain_terms, first_group, share_groups, 1)
    if backward:
        exchanged = jnp.flip(exchanged, 0)
    pieces = exchanged.reshape(ctx_devices, length, share_groups, GROUP)
    tables = modal_tables(own_rates, own_gains, length)
    block_decay = jnp.exp(-own_rates * length)[:, :, None]

    def advance(carried, piece):
        local_part, end_state = modal_block(piece, tables)
        result = local_part + jnp.einsum("tog,ogc->tgc", tables[1], carried, precision=exact_mode)
        return (block_decay * carried + end_state, result)

    start_state = jnp.zeros((ORDER, share_groups, GROUP), jnp.float32)
    _, block_outs = lax.scan(advance, start_state, pieces)
    whole_out = block_outs.reshape(ctx_devices * length, share_groups, GROUP)
    if backward:
        whole_out = jnp.flip(whole_out, 0)
    returned = lax.all_to_all(
        whole_out.astype(jnp.bfloat16), "ctx", split_axis=0, concat_axis=1, tiled=True
    ).astype(whole_out.dtype)
    return returned.reshape(length, channels)


def body(token_ids, embed_table, in_weight, feat_taps, modal_rates, modal_residues, out_grad):
    length = token_ids.shape[0]
    vocab_size = embed_table.shape[0]
    model_width = in_weight.shape[0]
    channels = in_weight.shape[2]
    flat_weight = in_weight.reshape(model_width, 3 * channels)
    one_hot = (token_ids[:, None] == jnp.arange(vocab_size, dtype=jnp.int32)[None, :]).astype(
        jnp.bfloat16
    )
    own_features = jnp.dot(one_hot, embed_table, preferred_element_type=jnp.float32).astype(
        jnp.bfloat16
    )
    rows_used = flat_weight
    projected = jnp.dot(
        lax.all_gather(own_features, "chan", axis=1, tiled=True),
        rows_used,
        preferred_element_type=jnp.float32,
    )
    stream = projected.reshape(length, 3, channels).astype(jnp.bfloat16)
    stream = lax.optimization_barrier(stream)
    featured = featurize_local(stream, feat_taps)
    query_rows = featured[:, 0]
    key_rows = featured[:, 1]
    value_rows = featured[:, 2]
    mixed_rows = key_rows * value_rows
    long_conv = modal_apply(mixed_rows, modal_rates, modal_residues, False)
    output = (query_rows * long_conv).astype(jnp.bfloat16)
    grad_rows = out_grad.astype(jnp.float32)
    grad_query = grad_rows * long_conv
    grad_long = grad_rows * query_rows
    grad_mixed = modal_apply(grad_long, modal_rates, modal_residues, True)
    grad_feat = jnp.stack(
        [grad_query, grad_mixed * value_rows, grad_mixed * key_rows], axis=1
    ).astype(jnp.bfloat16)
    grad_feat = lax.optimization_barrier(grad_feat)
    grad_proj = (
        featurize_back(grad_feat, feat_taps).astype(jnp.bfloat16).reshape(length, 3 * channels)
    )
    rows_used = flat_weight
    summed_rows = lax.psum_scatter(
        lax.dot_general(
            rows_used, grad_proj, (((1,), (1,)), ((), ())), preferred_element_type=jnp.float32
        ).astype(jnp.bfloat16),
        "chan",
        scatter_dimension=0,
        tiled=True,
    ).astype(jnp.float32)
    return (output, summed_rows.T.astype(jnp.bfloat16))


def solution(mesh):
    in_specs = (
        P("ctx"),
        P(None, "chan"),
        P(None, None, "chan"),
        P(None, None, "chan"),
        P(None, "chan"),
        P(None, "chan"),
        P("ctx", "chan"),
    )
    out_specs = (P("ctx", "chan"), P("ctx", "chan"))
    return jax.shard_map(body, mesh=mesh, in_specs=in_specs, out_specs=out_specs, check_vma=False)
```

profile of v0, /device:TPU:8, one launch (start us, length us, event | category | flops | bytes accessed | tf_op | source)
XLA Modules:
  0.0 326.2 jit_solution(7893675662903279602)
XLA Ops:
  7.2 0.9 copy-done
  8.1 1.6 convolution_convert_fusion
  9.8 0.8 constant_dynamic-slice_fusion.1
  10.7 16.7 %copy.55 = bf16[8192,3,256]{0,2,1:T(8,128)(2,1)} copy(bf16[8192,3,256]{2,0,1:T(8,128)(2,1)} %param.13) | data formatting | bytes 25165824 | tf_op args[2]
  27.5 58.0 %all-gather.2.cloned.1.call-done = bf16[256,8192]{1,0:T(8,128)(2,1)} async-done(((bf16[256,256]{1,0:T(8,128)(2,1)}), bf16[256,8192]{1,0:T(8,128)(2,1)}) %all-gather.2.cloned.1.call-update) | async-done | bytes 4194320 | tf_op jit(solution)/shard_map/all_gather | solution.py:114
  85.5 9.3 %fusion.58 = bf16[256,3,256]{2,0,1:T(8,128)(2,1)S(1)} fusion(bf16[8192,3,256]{0,2,1:T(8,128)(2,1)} %copy.55, bf16[256,8192]{1,0:T(8,128)(2,1)} %all-gather.2.cloned.1.call-done), kind=kOutput, calls=%fused_computation.61 | convolution fusion | flops 3221422080 | bytes 17170432 | tf_op jit(solution)/shard_map/dot_general | solution.py:113
  94.8 4.9 %collective-permute-start = (bf16[2,3,256]{2,0,1:T(2,128)(2,1)S(1)}, bf16[2,3,256]{2,0,1:T(2,128)(2,1)S(1)}, u32[]{:S(2)}, u32[]{:S(2)}) collective-permute-start(bf16[2,3,256]{2,0,1:T(2,128)(2,1)S(1)} %slice.59), channel_id=1, source_target_pairs={{0,32},{32,64},{64,96},{96,128},{128,160},{160,192},{192,224},{1,3... | collective-permute-start | bytes 9224 | tf_op jit(solution)/shard_map/ppermute | solution.py:15
  99.7 3.0 collective-permute-done
  103.9 6.3 %all-to-all-start.2 = ((bf16[256,16,16]{0,2,1:T(8,128)(2,1)}), bf16[256,16,16]{0,2,1:T(8,128)(2,1)S(1)}, u32[]{:S(2)}, u32[]{:S(2)}) async-start(bf16[256,16,16]{0,2,1:T(8,128)(2,1)} %bitcast.14), calls=%async_computation.2 | async-start | bytes 262144 | tf_op jit(solution)/shard_map/all_to_all | solution.py:72
  111.1 5.6 %all-to-all-done.2 = bf16[256,16,16]{0,2,1:T(8,128)(2,1)S(1)} async-done(((bf16[256,16,16]{0,2,1:T(8,128)(2,1)}), bf16[256,16,16]{0,2,1:T(8,128)(2,1)S(1)}, u32[]{:S(2)}, u32[]{:S(2)}) %all-to-all-start.2) | async-done | bytes 131104 | tf_op jit(solution)/shard_map/all_to_all | solution.py:72
  116.9 1.2 rev.7
  118.2 10.2 %while.31 = (s32[]{:T(128)}, f32[16,2,16]{0,2,1:T(8,128)S(1)}, bf16[8,256,2,16]{1,0,3,2:T(8,128)(2,1)S(1)}, f32[16,2,1]{0,1,2:T(2,128)S(1)}, f32[8,256,2,16]{1,0...) while((s32[]{:T(128)}, f32[16,2,16]{0,2,1:T(8,128)S(1)}, ...), condition=%wide.region_3.4_spmd.clone.clone.clone, body=%wide.region_2.3_spmd.clone.clone.clone.sunk | while | flops 28362756 | bytes 811800 | solution.py:90
  128.4 1.3 rev.8
  130.5 1.1 reshape.99
  131.6 10.6 %all_to_all.16 = bf16[8,2,4096]{2,1,0:T(2,128)(2,1)S(1)} all-to-all(bf16[8,2,4096]{2,1,0:T(2,128)(2,1)S(1)} %reshape.99), channel_id=1, replica_groups=mesh['ctx'=8,'chan'=32] {'ctx'}, dimensions={0} | all-to-all | bytes 262144 | tf_op jit(solution)/shard_map/all_to_all | solution.py:94
  144.8 4.9 %all-to-all-start = ((bf16[256,16,16]{0,2,1:T(8,128)(2,1)}), bf16[256,16,16]{0,2,1:T(8,128)(2,1)S(1)}, u32[]{:S(2)}, u32[]{:S(2)}) async-start(bf16[256,16,16]{0,2,1:T(8,128)(2,1)} %bitcast.6), calls=%async_computation | async-start | bytes 262144 | tf_op jit(solution)/shard_map/all_to_all | solution.py:72
  149.7 6.6 %all-to-all-done = bf16[256,16,16]{0,2,1:T(8,128)(2,1)S(1)} async-done(((bf16[256,16,16]{0,2,1:T(8,128)(2,1)}), bf16[256,16,16]{0,2,1:T(8,128)(2,1)S(1)}, u32[]{:S(2)}, u32[]{:S(2)}) %all-to-all-start) | async-done | bytes 131104 | tf_op jit(solution)/shard_map/all_to_all | solution.py:72
  156.3 8.4 %while.30 = (s32[]{:T(128)}, f32[16,2,16]{0,2,1:T(8,128)S(1)}, bf16[8,256,2,16]{1,3,2,0:T(8,128)(2,1)S(1)}, f32[16,2,1]{0,1,2:T(2,128)S(1)}, f32[8,256,2,16]{1,3...) while((s32[]{:T(128)}, f32[16,2,16]{0,2,1:T(8,128)S(1)}, ...), condition=%wide.region_1.2_spmd.clone.clone.clone, body=%wide.region_0.1_spmd.clone.clone.clone.sunk | while | flops 28354564 | bytes 730268 | solution.py:90
  165.4 1.1 reshape.97
  166.5 10.6 %all_to_all.17 = bf16[8,2,4096]{2,1,0:T(2,128)(2,1)S(1)} all-to-all(bf16[8,2,4096]{2,1,0:T(2,128)(2,1)S(1)} %reshape.97), channel_id=1, replica_groups=mesh['ctx'=8,'chan'=32] {'ctx'}, dimensions={0} | all-to-all | bytes 262144 | tf_op jit(solution)/shard_map/all_to_all | solution.py:94
  179.5 3.7 %collective-permute-start.1 = (bf16[2,3,256]{2,0,1:T(2,128)(2,1)S(1)}, bf16[2,3,256]{2,0,1:T(2,128)(2,1)S(1)}, u32[]{:S(2)}, u32[]{:S(2)}) collective-permute-start(bf16[2,3,256]{2,0,1:T(2,128)(2,1)S(1)} %slice.66), channel_id=1, source_target_pairs={{32,0},{64,32},{96,64},{128,96},{160,128},{192,160},{224,192},{33,... | collective-permute-start | bytes 9224 | tf_op jit(solution)/shard_map/ppermute | solution.py:15
  183.3 3.3 %collective-permute-done.1 = bf16[2,3,256]{2,0,1:T(2,128)(2,1)S(1)} collective-permute-done((bf16[2,3,256]{2,0,1:T(2,128)(2,1)S(1)}, bf16[2,3,256]{2,0,1:T(2,128)(2,1)S(1)}, u32[]{:S(2)}, u32[]{:S(2)}) %collective-permute-start.1) | collective-permute-done | bytes 3104 | tf_op jit(solution)/shard_map/ppermute | solution.py:15
  186.6 14.1 %fusion.56 = bf16[8192,256]{0,1:T(8,128)(2,1)} fusion(bf16[8192,3,256]{2,0,1:T(8,128)(2,1)} %param.13, f32[258,3,256]{2,0,1:T(8,128)S(1)} %maximum_convert_fusion.1, f32[3,256]{1,0:T(4,128)S(1)} %get-tuple-element.441, f32[3,256]{1,0:T(4,128)S(1)} %get-tuple-element.442, f32[3,256]{1,0:T(4,128)S(1)} %bitcast.160), kind=kOutput, calls=%fused_computation.59 | convolution fusion | flops 3224502272 | bytes 19148800 | tf_op jit(solution)/shard_map/dot_general | solution.py:140
  200.7 118.7 %reduce-scatter.2.cloned.1.call-done = bf16[256,256]{0,1:T(8,128)(2,1)} async-done(((bf16[8192,256]{0,1:T(8,128)(2,1)}), bf16[256,256]{0,1:T(8,128)(2,1)}) %reduce-scatter.2.cloned.1.call-update) | async-done | bytes 131088 | tf_op jit(solution)/shard_map/reduce_scatter | solution.py:139
  (125 shorter events, 27.0 us)
Async XLA Ops:
  7.2 1.0 copy-start
  7.2 78.3 %all-gather.2.cloned.1.call-start = ((), (), s32[]{:S(2)}) async-start(), calls=%async_computation.5 | async-start | bytes 4325376 | tf_op jit(solution)/shard_map/all_gather | solution.py:114
  10.7 16.8 %copy-start.2 = (f32[3,3,256]{2,1,0:T(4,128)S(1)}, f32[3,3,256]{2,1,0:T(4,128)}, u32[]{:S(2)}) copy-start(f32[3,3,256]{2,1,0:T(4,128)} %param.14) | copy-start | bytes 27652
  27.5 75.6 %copy-start.1 = (bf16[256,256]{1,0:T(8,128)(2,1)S(1)}, bf16[256,256]{1,0:T(8,128)(2,1)}, u32[]{:S(2)}) copy-start(bf16[256,256]{1,0:T(8,128)(2,1)} %param.17) | copy-start | bytes 393220
  94.8 7.9 %collective-permute-start = (bf16[2,3,256]{2,0,1:T(2,128)(2,1)S(1)}, bf16[2,3,256]{2,0,1:T(2,128)(2,1)S(1)}, u32[]{:S(2)}, u32[]{:S(2)}) collective-permute-start(bf16[2,3,256]{2,0,1:T(2,128)(2,1)S(1)} %slice.59), channel_id=1, source_target_pairs={{0,32},{32,64},{64,96},{96,128},{128,160},{160,192},{192,224},{1,3... | collective-permute-start | bytes 9224 | tf_op jit(solution)/shard_map/ppermute | solution.py:15
  103.9 12.9 %all-to-all-start.2 = ((bf16[256,16,16]{0,2,1:T(8,128)(2,1)}), bf16[256,16,16]{0,2,1:T(8,128)(2,1)S(1)}, u32[]{:S(2)}, u32[]{:S(2)}) async-start(bf16[256,16,16]{0,2,1:T(8,128)(2,1)} %bitcast.14), calls=%async_computation.2 | async-start | bytes 262144 | tf_op jit(solution)/shard_map/all_to_all | solution.py:72
  144.8 11.5 %all-to-all-start = ((bf16[256,16,16]{0,2,1:T(8,128)(2,1)}), bf16[256,16,16]{0,2,1:T(8,128)(2,1)S(1)}, u32[]{:S(2)}, u32[]{:S(2)}) async-start(bf16[256,16,16]{0,2,1:T(8,128)(2,1)} %bitcast.6), calls=%async_computation | async-start | bytes 262144 | tf_op jit(solution)/shard_map/all_to_all | solution.py:72
  149.7 169.7 %reduce-scatter.2.cloned.1.call-start = ((), (), s32[]{:S(2)}) async-start(), calls=%async_computation.6 | async-start | bytes 4325376 | tf_op jit(solution)/shard_map/reduce_scatter | solution.py:139
  179.5 7.0 %collective-permute-start.1 = (bf16[2,3,256]{2,0,1:T(2,128)(2,1)S(1)}, bf16[2,3,256]{2,0,1:T(2,128)(2,1)S(1)}, u32[]{:S(2)}, u32[]{:S(2)}) collective-permute-start(bf16[2,3,256]{2,0,1:T(2,128)(2,1)S(1)} %slice.66), channel_id=1, source_target_pairs={{32,0},{64,32},{96,64},{128,96},{160,128},{192,160},{224,192},{33,... | collective-permute-start | bytes 9224 | tf_op jit(solution)/shard_map/ppermute | solution.py:15
Sparse Core Ops, SparseCore 0:
  10.4 75.1 all-gather.1
  200.8 118.5 reduce-scatter.1
where the time goes:
time: 327 us; the launch traced here: 326 us
  waiting for transfers between devices  195 us (60%)
  matrix products  41.9 us (13%)
  local copies, waits for them, and re-layouts  31.7 us (10%)
  blocking collectives  21.2 us (6%)
  starting transfers between devices  19.9 us (6%)
  between operations  14.4 us (4%)
    reduce_scatter x1, waiting for transfers between devices, body(): lax.psum_scatter(lax.dot_general(rows_used, grad_proj, (((1,), (1,)), (()...  119 us
    all_gather x1, waiting for transfers between devices, body(): lax.all_gather(own_features, 'chan', axis=1, tiled=True)  58 us
    unnamed x19, local copies, waits for them, and re-layouts  21.8 us
    all_to_all x2, blocking collectives, modal_apply(): lax.all_to_all(whole_out.astype(jnp.bfloat16), 'ctx', split_axis=0, conca...  21.2 us
    dot_general x1, matrix products, body(): lax.dot_general(rows_used, grad_proj, (((1,), (1,)), ((), ())), preferred...  14.1 us
    all_to_all x2, waiting for transfers between devices, modal_apply(): lax.all_to_all(shaped.astype(jnp.bfloat16), 'ctx', split_axis=1, concat_a...  12.2 us
    all_to_all x2, starting transfers between devices, modal_apply(): lax.all_to_all(shaped.astype(jnp.bfloat16), 'ctx', split_axis=1, concat_a...  11.2 us
    dot_general x1, matrix products, body(): jnp.dot(lax.all_gather(own_features, 'chan', axis=1, tiled=True), rows_us...  9.3 us
  transfers between devices with their start and end apart: 6, of which 6 were waited for; matrix products, arithmetic and copies ran while one was open for 6% of the time, Pallas kernels for 0%

commit v1 on v0

--- a/solution.py
+++ b/solution.py
@@ -111,7 +111,9 @@
     )
     rows_used = flat_weight
     projected = jnp.dot(
-        lax.all_gather(own_features, "chan", axis=1, tiled=True),
+        jnp.concatenate(
+            lax.all_to_all(jnp.stack([own_features] * lax.axis_size("chan")), "chan", 0, 0), axis=1
+        ),
         rows_used,
         preferred_element_type=jnp.float32,
     )

time: 327 us -> 373 us (1.14)
  waiting for transfers between devices: 195 us -> 217 us
  local copies, waits for them, and re-layouts: 31.7 us -> 47.2 us
  starting transfers between devices: 19.9 us -> 29.4 us
    all_to_all x0 -> x1, waiting for transfers between devices: none -> 78.3 us  [body(): lax.all_to_all(jnp.stack([own_features] * lax.axis_size('chan')), 'chan',...]
    all_gather x1 -> x0, waiting for transfers between devices: 58 us -> none  [body(): lax.all_gather(own_features, 'chan', axis=1, tiled=True)]
    reshape x0 -> x2, local copies, waits for them, and re-layouts: none -> 13.9 us  [body(): jnp.concatenate(lax.all_to_all(jnp.stack([own_features] * lax.axis_size('...]
    all_to_all x0 -> x1, starting transfers between devices: none -> 9.91 us  [body(): lax.all_to_all(jnp.stack([own_features] * lax.axis_size('chan')), 'chan',...]
    unnamed x19 -> x23, local copies, waits for them, and re-layouts: 21.8 us -> 21.7 us
  transfers between devices with their start and end apart: 6 -> 6, of which waited for: 6 -> 6; matrix products, arithmetic and copies ran while one was open for 6% -> 5% of each run, Pallas kernels for 0% -> 0%
where the time goes in v1:
time: 373 us; the launch traced here: 372 us
  waiting for transfers between devices  217 us (58%)
  local copies, waits for them, and re-layouts  47.2 us (13%)
  matrix products  41.2 us (11%)
  starting transfers between devices  29.4 us (8%)
  blocking collectives  21.2 us (6%)
  between operations  14.4 us (4%)
    reduce_scatter x1, waiting for transfers between devices, body(): lax.psum_scatter(lax.dot_general(rows_used, grad_proj, (((1,), (1,)), (()...  120 us
    all_to_all x1, waiting for transfers between devices, body(): lax.all_to_all(jnp.stack([own_features] * lax.axis_size('chan')), 'chan',...  78.3 us
    unnamed x23, local copies, waits for them, and re-layouts  21.7 us
    all_to_all x2, blocking collectives, modal_apply(): lax.all_to_all(whole_out.astype(jnp.bfloat16), 'ctx', split_axis=0, conca...  21.2 us
    dot_general x1, matrix products, body(): lax.dot_general(rows_used, grad_proj, (((1,), (1,)), ((), ())), preferred...  14.1 us
    reshape x2, local copies, waits for them, and re-layouts, body(): jnp.concatenate(lax.all_to_all(jnp.stack([own_features] * lax.axis_size('...  13.9 us
    all_to_all x2, waiting for transfers between devices, modal_apply(): lax.all_to_all(shaped.astype(jnp.bfloat16), 'ctx', split_axis=1, concat_a...  12.2 us
    all_to_all x2, starting transfers between devices, modal_apply(): lax.all_to_all(shaped.astype(jnp.bfloat16), 'ctx', split_axis=1, concat_a...  11.1 us
  transfers between devices with their start and end apart: 6, of which 6 were waited for; matrix products, arithmetic and copies ran while one was open for 5% of the time, Pallas kernels for 0%

profile of v1, /device:TPU:8, one launch (start us, length us, event | category | flops | bytes accessed | tf_op | source)
XLA Modules:
  0.0 372.2 jit_solution(8570081349677935740)
XLA Ops:
  9.1 2.4 stack.8
  11.5 9.9 %all-to-all-start = ((bf16[32,256,256]{2,1,0:T(8,128)(2,1)}), bf16[32,256,256]{2,1,0:T(8,128)(2,1)}, u32[]{:S(2)}, u32[]{:S(2)}) async-start(bf16[32,256,256]{2,1,0:T(8,128)(2,1)} %stack.8), calls=%async_computation | async-start | bytes 8388608 | tf_op jit(solution)/shard_map/all_to_all | solution.py:115
  21.7 16.6 %copy.57 = bf16[8192,3,256]{0,2,1:T(8,128)(2,1)} copy(bf16[8192,3,256]{2,0,1:T(8,128)(2,1)} %param.13) | data formatting | bytes 25165824 | tf_op args[2]
  38.4 78.3 %all-to-all-done = bf16[32,256,256]{2,1,0:T(8,128)(2,1)} async-done(((bf16[32,256,256]{2,1,0:T(8,128)(2,1)}), bf16[32,256,256]{2,1,0:T(8,128)(2,1)}, u32[]{:S(2)}, u32[]{:S(2)}) %all-to-all-start) | async-done | bytes 4194336 | tf_op jit(solution)/shard_map/all_to_all | solution.py:115
  116.7 6.5 %copy.56 = bf16[256,32,256]{2,1,0:T(8,128)(2,1)} copy(bf16[256,32,256]{2,0,1:T(8,128)(2,1)} %bitcast) | data formatting | bytes 8388608 | tf_op jit(solution)/shard_map/reshape | solution.py:114
  123.2 7.4 %reshape.105 = bf16[256,8192,1]{1,0,2:T(8,128)(2,1)} reshape(bf16[256,32,256]{2,1,0:T(8,128)(2,1)} %copy.56) | data formatting | bytes 8388608 | tf_op jit(solution)/shard_map/reshape | solution.py:114
  130.6 9.3 %fusion.57 = bf16[256,3,256]{2,0,1:T(8,128)(2,1)S(1)} fusion(bf16[256,8192,1]{1,0,2:T(8,128)(2,1)} %reshape.105, bf16[8192,3,256]{0,2,1:T(8,128)(2,1)} %copy.57), kind=kOutput, calls=%fused_computation.60 | convolution fusion | flops 3221422080 | bytes 17170432 | tf_op jit(solution)/shard_map/dot_general | solution.py:113
  140.0 4.6 %collective-permute-start = (bf16[2,3,256]{2,0,1:T(2,128)(2,1)S(1)}, bf16[2,3,256]{2,0,1:T(2,128)(2,1)S(1)}, u32[]{:S(2)}, u32[]{:S(2)}) collective-permute-start(bf16[2,3,256]{2,0,1:T(2,128)(2,1)S(1)} %slice.59), channel_id=1, source_target_pairs={{0,32},{32,64},{64,96},{96,128},{128,160},{160,192},{192,224},{1,3... | collective-permute-start | bytes 9224 | tf_op jit(solution)/shard_map/ppermute | solution.py:15
  144.6 3.2 collective-permute-done
  149.0 6.2 %all-to-all-start.3 = ((bf16[256,16,16]{0,2,1:T(8,128)(2,1)}), bf16[256,16,16]{0,2,1:T(8,128)(2,1)S(1)}, u32[]{:S(2)}, u32[]{:S(2)}) async-start(bf16[256,16,16]{0,2,1:T(8,128)(2,1)} %bitcast.14), calls=%async_computation.3 | async-start | bytes 262144 | tf_op jit(solution)/shard_map/all_to_all | solution.py:72
  156.1 5.6 %all-to-all-done.3 = bf16[256,16,16]{0,2,1:T(8,128)(2,1)S(1)} async-done(((bf16[256,16,16]{0,2,1:T(8,128)(2,1)}), bf16[256,16,16]{0,2,1:T(8,128)(2,1)S(1)}, u32[]{:S(2)}, u32[]{:S(2)}) %all-to-all-start.3) | async-done | bytes 131104 | tf_op jit(solution)/shard_map/all_to_all | solution.py:72
  161.9 1.2 rev.7
  163.2 10.2 %while.31 = (s32[]{:T(128)}, f32[16,2,16]{0,2,1:T(8,128)S(1)}, bf16[8,256,2,16]{1,0,3,2:T(8,128)(2,1)S(1)}, f32[16,2,1]{0,1,2:T(2,128)S(1)}, f32[8,256,2,16]{1,0...) while((s32[]{:T(128)}, f32[16,2,16]{0,2,1:T(8,128)S(1)}, ...), condition=%wide.region_3.4_spmd.clone.clone.clone, body=%wide.region_2.3_spmd.clone.clone.clone.sunk | while | flops 28362756 | bytes 811800 | solution.py:90
  173.4 1.3 rev.8
  175.5 1.1 reshape.110
  176.5 10.6 %all_to_all.20 = bf16[8,2,4096]{2,1,0:T(2,128)(2,1)S(1)} all-to-all(bf16[8,2,4096]{2,1,0:T(2,128)(2,1)S(1)} %reshape.110), channel_id=1, replica_groups=mesh['ctx'=8,'chan'=32] {'ctx'}, dimensions={0} | all-to-all | bytes 262144 | tf_op jit(solution)/shard_map/all_to_all | solution.py:94
  189.7 4.9 %all-to-all-start.1 = ((bf16[256,16,16]{0,2,1:T(8,128)(2,1)}), bf16[256,16,16]{0,2,1:T(8,128)(2,1)S(1)}, u32[]{:S(2)}, u32[]{:S(2)}) async-start(bf16[256,16,16]{0,2,1:T(8,128)(2,1)} %bitcast.6), calls=%async_computation.1 | async-start | bytes 262144 | tf_op jit(solution)/shard_map/all_to_all | solution.py:72
  194.6 6.6 %all-to-all-done.1 = bf16[256,16,16]{0,2,1:T(8,128)(2,1)S(1)} async-done(((bf16[256,16,16]{0,2,1:T(8,128)(2,1)}), bf16[256,16,16]{0,2,1:T(8,128)(2,1)S(1)}, u32[]{:S(2)}, u32[]{:S(2)}) %all-to-all-start.1) | async-done | bytes 131104 | tf_op jit(solution)/shard_map/all_to_all | solution.py:72
  201.2 8.4 %while.30 = (s32[]{:T(128)}, f32[16,2,16]{0,2,1:T(8,128)S(1)}, bf16[8,256,2,16]{1,3,2,0:T(8,128)(2,1)S(1)}, f32[16,2,1]{0,1,2:T(2,128)S(1)}, f32[8,256,2,16]{1,3...) while((s32[]{:T(128)}, f32[16,2,16]{0,2,1:T(8,128)S(1)}, ...), condition=%wide.region_1.2_spmd.clone.clone.clone, body=%wide.region_0.1_spmd.clone.clone.clone.sunk | while | flops 28354564 | bytes 730268 | solution.py:90
  211.4 10.6 %all_to_all.42 = bf16[8,2,4096]{2,1,0:T(2,128)(2,1)S(1)} all-to-all(bf16[8,2,4096]{2,1,0:T(2,128)(2,1)S(1)} %reshape.108), channel_id=1, replica_groups=mesh['ctx'=8,'chan'=32] {'ctx'}, dimensions={0} | all-to-all | bytes 262144 | tf_op jit(solution)/shard_map/all_to_all | solution.py:94
  224.5 3.7 collective-permute-start.1
  228.2 3.3 collective-permute-done.1
  231.5 14.1 %fusion.56 = bf16[8192,256]{0,1:T(8,128)(2,1)} fusion(bf16[8192,3,256]{2,0,1:T(8,128)(2,1)} %param.13, f32[258,3,256]{2,0,1:T(8,128)S(1)} %maximum_convert_fusion.1, f32[3,256]{1,0:T(4,128)S(1)} %get-tuple-element.441, f32[3,256]{1,0:T(4,128)S(1)} %get-tuple-element.442, f32[3,256]{1,0:T(4,128)S(1)} %bitcast.157), kind=kOutput, calls=%fused_computation.59 | convolution fusion | flops 3224502272 | bytes 19148800 | tf_op jit(solution)/shard_map/dot_general | solution.py:142
  245.6 119.8 %reduce-scatter.2.cloned.1.call-done = bf16[256,256]{0,1:T(8,128)(2,1)} async-done(((bf16[8192,256]{0,1:T(8,128)(2,1)}), bf16[256,256]{0,1:T(8,128)(2,1)}) %reduce-scatter.2.cloned.1.call-update) | async-done | bytes 131088 | tf_op jit(solution)/shard_map/reduce_scatter | solution.py:141
  (131 shorter events, 29.9 us)
Async XLA Ops:
  7.2 1.0 copy-start
  7.2 14.2 %copy-start.2 = (f32[16,16]{1,0:T(8,128)S(1)}, f32[16,16]{1,0:T(8,128)}, u32[]{:S(2)}) copy-start(f32[16,16]{1,0:T(8,128)} %param.16) | copy-start | bytes 3076
  7.2 14.2 %copy-start.3 = (f32[16,16]{1,0:T(8,128)S(1)}, f32[16,16]{1,0:T(8,128)}, u32[]{:S(2)}) copy-start(f32[16,16]{1,0:T(8,128)} %param.15) | copy-start | bytes 3076
  11.5 105.2 %all-to-all-start = ((bf16[32,256,256]{2,1,0:T(8,128)(2,1)}), bf16[32,256,256]{2,1,0:T(8,128)(2,1)}, u32[]{:S(2)}, u32[]{:S(2)}) async-start(bf16[32,256,256]{2,1,0:T(8,128)(2,1)} %stack.8), calls=%async_computation | async-start | bytes 8388608 | tf_op jit(solution)/shard_map/all_to_all | solution.py:115
  21.7 16.7 %copy-start.4 = (f32[3,3,256]{2,1,0:T(4,128)S(1)}, f32[3,3,256]{2,1,0:T(4,128)}, u32[]{:S(2)}) copy-start(f32[3,3,256]{2,1,0:T(4,128)} %param.14) | copy-start | bytes 27652
  130.6 17.6 %copy-start.1 = (bf16[256,256]{1,0:T(8,128)(2,1)S(1)}, bf16[256,256]{1,0:T(8,128)(2,1)}, u32[]{:S(2)}) copy-start(bf16[256,256]{1,0:T(8,128)(2,1)} %param.17) | copy-start | bytes 393220
  140.0 7.9 %collective-permute-start = (bf16[2,3,256]{2,0,1:T(2,128)(2,1)S(1)}, bf16[2,3,256]{2,0,1:T(2,128)(2,1)S(1)}, u32[]{:S(2)}, u32[]{:S(2)}) collective-permute-start(bf16[2,3,256]{2,0,1:T(2,128)(2,1)S(1)} %slice.59), channel_id=1, source_target_pairs={{0,32},{32,64},{64,96},{96,128},{128,160},{160,192},{192,224},{1,3... | collective-permute-start | bytes 9224 | tf_op jit(solution)/shard_map/ppermute | solution.py:15
  149.0 12.7 %all-to-all-start.3 = ((bf16[256,16,16]{0,2,1:T(8,128)(2,1)}), bf16[256,16,16]{0,2,1:T(8,128)(2,1)S(1)}, u32[]{:S(2)}, u32[]{:S(2)}) async-start(bf16[256,16,16]{0,2,1:T(8,128)(2,1)} %bitcast.14), calls=%async_computation.3 | async-start | bytes 262144 | tf_op jit(solution)/shard_map/all_to_all | solution.py:72
  189.7 11.5 %all-to-all-start.1 = ((bf16[256,16,16]{0,2,1:T(8,128)(2,1)}), bf16[256,16,16]{0,2,1:T(8,128)(2,1)S(1)}, u32[]{:S(2)}, u32[]{:S(2)}) async-start(bf16[256,16,16]{0,2,1:T(8,128)(2,1)} %bitcast.6), calls=%async_computation.1 | async-start | bytes 262144 | tf_op jit(solution)/shard_map/all_to_all | solution.py:72
  194.6 170.8 %reduce-scatter.2.cloned.1.call-start = ((), (), s32[]{:S(2)}) async-start(), calls=%async_computation.6 | async-start | bytes 4325376 | tf_op jit(solution)/shard_map/reduce_scatter | solution.py:141
  224.5 7.0 %collective-permute-start.1 = (bf16[2,3,256]{2,0,1:T(2,128)(2,1)S(1)}, bf16[2,3,256]{2,0,1:T(2,128)(2,1)S(1)}, u32[]{:S(2)}, u32[]{:S(2)}) collective-permute-start(bf16[2,3,256]{2,0,1:T(2,128)(2,1)S(1)} %slice.66), channel_id=1, source_target_pairs={{32,0},{64,32},{96,64},{128,96},{160,128},{192,160},{224,192},{33,... | collective-permute-start | bytes 9224 | tf_op jit(solution)/shard_map/ppermute | solution.py:15
Sparse Core Ops, SparseCore 0:
  245.7 119.6 reduce-scatter.1
